TPU v7x, 32 devices: a whole 2x2x4 slice. The times are simulated.
32 devices in a mesh: tiles: 2 (over y), row: 8 (over z, x), col: 2 (over core).
Axes of the slice: x: 2, y: 2, z: 4, core: 2. Of those that a mesh axis runs over, the one named last changes fastest.
Arguments:
- layers: float32 [8, 4096, 4096], P('tiles', 'row', 'col'), parts along dimension 0, may hold values from -6 to 6
- unmixing: bfloat16 [4, 4, 4, 2048, 4096], P('tiles', None, None, ('row', 'col')), parts along dimension 0, may hold values from -2 to 2
Outputs:
- components: float32 [8, 4096, 4096], P('tiles', 'row', 'col'), parts along dimension 0
There are 2 independent parts, one for each index of `tiles`. A program takes and returns all parts, laid end to end along the dimension named above; each array names one. Nothing has to cross between parts.
All inputs are finite; a program needn't handle non-finite values.
Results may differ from a plain program's by a relative error of at most 0.0003.
Values sent between devices are 32-bit elements; how exact they have to be, the bound alone decides.
No kernel may reach another device: no remote copies, remote signals or barrier semaphores. Data moves between devices by JAX's collectives and lax.ppermute only.
A program may use at most 320 MiB of HBM per device.

v0:
```python
import math
import jax
import jax.numpy as jnp
from jax import lax
from jax.sharding import PartitionSpec as P


def phase_pair(first_len, second_len, period, sign):
    first = lax.broadcasted_iota(jnp.int32, (first_len, second_len), 0)
    second = lax.broadcasted_iota(jnp.int32, (first_len, second_len), 1)
    turns = (first * second % period).astype(jnp.float32)
    phase = turns * (sign * 2.0 * math.pi / period)
    return (jnp.cos(phase), jnp.sin(phase))


def contract_first(values, table):
    return jnp.einsum("...qp,qk->...pk", values, table, precision=lax.Precision.HIGHEST)


def contract_second(values, table):
    return jnp.einsum("...pk,pj->...jk", values, table, precision=lax.Precision.HIGHEST)


def fourier(real_in, imag_in, length, sign, in_len, out_len, real_only):
    inner_len = min(length, 128)
    outer_len = length // inner_len
    rows_in = in_len // outer_len
    rows_out = out_len // inner_len
    leading = real_in.shape[:-1]
    first_cos, first_sin = phase_pair(rows_in, inner_len, inner_len, sign)
    first_table = jnp.concatenate([first_cos, first_sin], axis=1)
    both = contract_first(real_in.reshape(leading + (rows_in, outer_len)), first_table)
    part_real = both[..., :inner_len]
    part_imag = both[..., inner_len:]
    if imag_in is not None:
        other = contract_first(imag_in.reshape(leading + (rows_in, outer_len)), first_table)
        part_real = part_real - other[..., inner_len:]
        part_imag = part_imag + other[..., :inner_len]
    twist_cos, twist_sin = phase_pair(outer_len, inner_len, length, sign)
    turned_real = part_real * twist_cos - part_imag * twist_sin
    turned_imag = part_real * twist_sin + part_imag * twist_cos
    stacked = jnp.concatenate([turned_real, turned_imag], axis=-2)
    second_cos, second_sin = phase_pair(outer_len, rows_out, outer_len, sign)
    table_real = jnp.concatenate([second_cos, -second_sin], axis=0)
    if real_only:
        result_real = contract_second(stacked, table_real)
        return result_real.reshape(leading + (out_len,))
    table_imag = jnp.concatenate([second_sin, second_cos], axis=0)
    combined = contract_second(stacked, jnp.concatenate([table_real, table_imag], axis=1))
    result_real = combined[..., :rows_out, :].reshape(leading + (out_len,))
    result_imag = combined[..., rows_out:, :].reshape(leading + (out_len,))
    return (result_real, result_imag)


def reorder_blocks(values, row_count, col_count):
    leading = values.shape[0]
    block = values.shape[1] // (row_count * col_count)
    width = values.shape[2]
    split = values.reshape(leading, col_count, row_count, block, width)
    return jnp.transpose(split, (0, 4, 2, 1, 3)).reshape(
        leading, width, row_count * col_count * block
    )


def shards(layers, unmixing):
    row_count = lax.axis_size("row")
    col_count = lax.axis_size("col")
    rows_len = layers.shape[1] * row_count
    cols_len = layers.shape[2] * col_count
    spec_real, spec_imag = fourier(
        lax.all_to_all(layers, "col", split_axis=1, concat_axis=2, tiled=True),
        None,
        cols_len,
        -1.0,
        cols_len,
        cols_len // 2,
        False,
    )
    moved_real, moved_imag = (
        lax.all_to_all(
            lax.all_to_all(spec_real, "row", split_axis=2, concat_axis=1, tiled=True),
            "col",
            split_axis=2,
            concat_axis=1,
            tiled=True,
        ),
        lax.all_to_all(
            lax.all_to_all(spec_imag, "row", split_axis=2, concat_axis=1, tiled=True),
            "col",
            split_axis=2,
            concat_axis=1,
            tiled=True,
        ),
    )
    line_real = reorder_blocks(moved_real, row_count, col_count)
    line_imag = reorder_blocks(moved_imag, row_count, col_count)
    wave_real, wave_imag = fourier(line_real, line_imag, rows_len, -1.0, rows_len, rows_len, False)
    mixed_real = None
    mixed_imag = None
    for layer_index in range(4):
        weight_real = unmixing[0, :, layer_index].astype(jnp.float32)
        weight_imag = unmixing[1, :, layer_index].astype(jnp.float32)
        layer_real = wave_real[layer_index][None]
        layer_imag = wave_imag[layer_index][None]
        term_real = weight_real * layer_real - weight_imag * layer_imag
        term_imag = weight_real * layer_imag + weight_imag * layer_real
        if mixed_real is None:
            mixed_real = term_real
            mixed_imag = term_imag
        else:
            mixed_real = mixed_real + term_real
            mixed_imag = mixed_imag + term_imag
    back_real, back_imag = fourier(mixed_real, mixed_imag, rows_len, 1.0, rows_len, rows_len, False)
    scale = 2.0 / (rows_len * cols_len)
    sent_real, sent_imag = (
        lax.all_to_all(
            lax.all_to_all(back_real, "row", split_axis=2, concat_axis=1, tiled=True),
            "col",
            split_axis=2,
            concat_axis=1,
            tiled=True,
        ),
        lax.all_to_all(
            lax.all_to_all(back_imag, "row", split_axis=2, concat_axis=1, tiled=True),
            "col",
            split_axis=2,
            concat_axis=1,
            tiled=True,
        ),
    )
    grid_real = reorder_blocks(sent_real, row_count, col_count)
    grid_imag = reorder_blocks(sent_imag, row_count, col_count)
    fields = fourier(grid_real, grid_imag, cols_len, 1.0, cols_len // 2, cols_len, True)
    fields = fields * scale
    return lax.all_to_all(fields, "col", split_axis=2, concat_axis=1, tiled=True)


def solution(mesh):
    in_specs = (P("tiles", "row", "col"), P("tiles", None, None, ("row", "col"), None))
    out_specs = P("tiles", "row", "col")
    return jax.shard_map(shards, mesh=mesh, in_specs=in_specs, out_specs=out_specs, check_vma=False)
```

profile of v0, /device:TPU:0, one launch (start us, length us, event | category | flops | bytes accessed | tf_op | source)
XLA Modules:
  0.0 1691.4 jit_solution(6777798758830967953)
XLA Ops:
  0.0 20.9 %copy.174 = f32[4,512,2048]{2,0,1:T(4,128)} copy(f32[4,512,2048]{2,1,0:T(8,128)} %param.2) | data formatting | bytes 33554432 | tf_op args[0]
  20.9 9.7 all-to-all-start
  31.2 12.9 all-to-all-done
  44.1 17.8 %copy.175 = f32[4,512,2048]{2,1,0:T(8,128)} copy(f32[4,512,2048]{2,0,1:T(4,128)} %all-to-all-done) | data formatting | bytes 33554432 | tf_op jit(solution)/shard_map/all_to_all | solution.py:71
  61.9 16.4 copy.176
  78.3 44.1 %fusion.8 = f32[4,256,32,256]{1,3,2,0:T(8,128)} fusion(f32[4,256,128,32]{1,3,2,0:T(8,128)} %bitcast.134, f32[128,128]{0,1:T(8,128)S(1)} %get-tuple-element.35, f32[128,128]{0,1:T(8,128)S(1)} %get-tuple-element.36), kind=kOutput, calls=%fused_computation.19 | convolution fusion | flops 12884934656 | bytes 50462720 | tf_op jit(solution)/shard_map/...qp,qk->...pk/dot_general | solution.py:17
  122.4 17.6 %multiply_subtract_fusion.1 = (f32[4,256,32,128]{1,3,2,0:T(8,128)S(1)}, f32[4,256,32,128]{1,3,2,0:T(8,128)}) fusion(f32[4,256,32,256]{1,3,2,0:T(8,128)} %fusion.8, f32[32,128]{1,0:T(8,128)S(1)} %get-tuple-element.37, f32[32,128]{1,0:T(8,128)S(1)} %get-tuple-element.38), kind=kLoop, calls=%fused_computation.18 | loop fusion | flops 25165824 | bytes 67141632 | tf_op jit(solution)/shard_map/sub | solution.py:40
  140.0 18.5 %pad_maximum_fusion = f32[4,256,64,128]{1,3,2,0:T(8,128)} fusion(f32[4,256,32,128]{1,3,2,0:T(8,128)} %get-tuple-element.14, f32[4,256,32,128]{1,3,2,0:T(8,128)S(1)} %get-tuple-element.13), kind=kLoop, calls=%fused_computation | loop fusion | flops 8388608 | bytes 67108864 | tf_op jit(solution)/shard_map/concatenate | solution.py:42
  158.5 31.8 %copy.178 = f32[4,256,64,128]{3,2,1,0:T(8,128)} copy(f32[4,256,64,128]{1,3,2,0:T(8,128)} %pad_maximum_fusion) | data formatting | bytes 67108864 | tf_op jit(solution)/shard_map/concatenate | solution.py:42
  190.3 24.1 %convolution_bitcast_fusion = f32[4,256,32,128]{3,2,1,0:T(8,128)S(1)} fusion(f32[4,256,64,128]{3,2,1,0:T(8,128)} %copy.178, f32[32,16]{0,1:T(8,128)S(1)} %get-tuple-element.40, f32[32,16]{0,1:T(8,128)S(1)} %get-tuple-element.39, f32[32,16]{0,1:T(8,128)S(1)} %fusion.98), kind=kOutput, calls=%fused_computation.36 | convolution fusion | flops 3221231616 | bytes 50337792 | tf_op jit(solution)/shard_map/...pk,pj->...jk/dot_general | solution.py:21
  221.4 8.1 copy.247
  236.7 8.0 copy.249
  244.7 175.5 %all-to-all-done.1 = f32[4,256,2048]{1,0,2:T(4,128)} async-done(((f32[4,256,2048]{1,0,2:T(4,128)}), f32[4,256,2048]{1,0,2:T(4,128)}, u32[]{:S(2)}, u32[]{:S(2)}) %all-to-all-start.1) | async-done | bytes 8388640 | tf_op jit(solution)/shard_map/all_to_all | solution.py:81
  420.2 8.3 copy.180
  428.4 8.7 copy.181
  437.2 10.4 copy.182
  447.6 18.5 %all_to_all.165 = f32[4,2048,256]{1,0,2:T(4,128)} all-to-all(f32[4,2048,256]{1,0,2:T(4,128)} %copy.182), channel_id=1, replica_groups=mesh['tiles'=2,'row'=8,'col'=2] {'col'}, dimensions={2} | all-to-all | bytes 16777216 | tf_op jit(solution)/shard_map/all_to_all | solution.py:80
  471.2 23.0 %fusion.110 = (bf16[1,4,1,128,4096]{4,3,2,1,0:T(8,128)(2,1)}, bf16[1,4,1,128,4096]{4,3,2,1,0:T(8,128)(2,1)}, bf16[1,4,1,128,4096]{4,3,2,1,0:T(8,128)(2,1)}, bf16...) fusion(bf16[2,4,4,128,4096]{4,3,2,1,0:T(8,128)(2,1)} %param.3), kind=kLoop, calls=%fused_computation.172 | loop fusion | bytes 67108864 | tf_op jit(solution)/shard_map/slice | solution.py:102
  547.6 11.5 copy.183
  559.1 8.7 copy.184
  571.8 19.7 %fusion.43 = f32[4,128,32,256]{3,1,2,0:T(8,128)} fusion(f32[4,128,128,32]{1,3,2,0:T(8,128)S(1)} %bitcast.133, f32[128,128]{0,1:T(8,128)S(1)} %copy-done.1, f32[128,128]{0,1:T(8,128)S(1)} %copy-done.3), kind=kOutput, calls=%fused_computation.67 | convolution fusion | flops 6442483712 | bytes 25296896 | tf_op jit(solution)/shard_map/...qp,qk->...pk/dot_general | solution.py:17
  591.5 63.4 %all-to-all-done.3 = f32[4,256,2048]{1,0,2:T(4,128)} async-done(((f32[4,256,2048]{1,0,2:T(4,128)}), f32[4,256,2048]{1,0,2:T(4,128)}, u32[]{:S(2)}, u32[]{:S(2)}) %all-to-all-start.3) | async-done | bytes 8388640 | tf_op jit(solution)/shard_map/all_to_all | solution.py:88
  654.9 8.4 copy.189
  663.2 8.7 copy.190
  672.0 10.4 copy.191
  682.3 12.5 all_to_all.166
  694.8 8.3 copy.192
  703.1 8.7 copy.193
  715.7 19.5 %fusion.41 = f32[4,128,32,256]{3,1,2,0:T(8,128)} fusion(f32[4,128,128,32]{1,3,2,0:T(8,128)S(1)} %bitcast.132, f32[128,128]{0,1:T(8,128)S(1)} %copy-done.1, f32[128,128]{0,1:T(8,128)S(1)} %copy-done.3), kind=kOutput, calls=%fused_computation.65 | convolution fusion | flops 6442483712 | bytes 25296896 | tf_op jit(solution)/shard_map/...qp,qk->...pk/dot_general | solution.py:17
  735.2 19.1 %multiply_subtract_fusion.3 = (f32[4,128,32,128]{3,1,2,0:T(8,128)}, f32[4,128,32,128]{3,1,2,0:T(8,128)}) fusion(f32[32,128]{1,0:T(8,128)S(1)} %copy-done.11, f32[32,128]{1,0:T(8,128)S(1)} %copy-done.13, f32[4,128,32,256]{3,1,2,0:T(8,128)} %fusion.41, f32[4,128,32,256]{3,1,2,0:T(8,128)} %fusion.43), kind=kLoop, calls=%fused_computation.72 | loop fusion | flops 16777216 | bytes 50364416 | tf_op jit(solution)/shard_map/sub | solution.py:40
  754.3 11.9 pad_maximum_fusion.2
  766.2 33.5 %fusion.11 = f32[4,128,64,128]{3,2,1,0:T(8,128)} fusion(f32[4,128,64,128]{3,1,2,0:T(8,128)} %pad_maximum_fusion.2, f32[32,32]{0,1:T(8,128)S(1)} %get-tuple-element.42, f32[32,32]{0,1:T(8,128)S(1)} %get-tuple-element.41, f32[32,32]{0,1:T(8,128)S(1)} %fusion.95), kind=kOutput, calls=%fused_computation.37 | convolution fusion | flops 3221237760 | bytes 33566720 | tf_op jit(solution)/shard_map/...pk,pj->...jk/dot_general | solution.py:21
  799.7 12.3 fusion.112
  834.9 17.6 %fusion.22 = (f32[4,128,128,32]{1,3,2,0:T(8,128)S(1)}, f32[4,128,128,32]{1,3,2,0:T(8,128)S(1)}) fusion(bf16[4,128,128,32]{1,3,2,0:T(8,128)(2,1)} %bitcast.169, bf16[4,128,128,32]{1,3,2,0:T(8,128)(2,1)} %bitcast.168, bf16[4,128,128,32]{1,3,2,0:T(8,128)(2,1)} %bitcast.167, bf16[4,128,128,32]{1,3,2,0:T(8,128)(2,1)} %bitcast.166, ...), kind=kLoop, calls=%fused_computation.42 | loop fusion | flops 79691776 | bytes 67108864 | tf_op jit(solution)/shard_map/add | solution.py:111
  852.5 19.4 %fusion.39 = f32[4,128,32,256]{3,1,2,0:T(8,128)} fusion(f32[4,128,128,32]{1,3,2,0:T(8,128)S(1)} %get-tuple-element.7, f32[128,128]{0,1:T(8,128)S(1)} %get-tuple-element.43, f32[128,128]{0,1:T(8,128)S(1)} %get-tuple-element.44), kind=kOutput, calls=%fused_computation.63 | convolution fusion | flops 6442483712 | bytes 25296896 | tf_op jit(solution)/shard_map/...qp,qk->...pk/dot_general | solution.py:17
  872.0 19.5 %fusion.37 = f32[4,128,32,256]{3,1,2,0:T(8,128)} fusion(f32[4,128,128,32]{1,3,2,0:T(8,128)S(1)} %get-tuple-element.8, f32[128,128]{0,1:T(8,128)S(1)} %get-tuple-element.43, f32[128,128]{0,1:T(8,128)S(1)} %get-tuple-element.44), kind=kOutput, calls=%fused_computation.61 | convolution fusion | flops 6442483712 | bytes 25296896 | tf_op jit(solution)/shard_map/...qp,qk->...pk/dot_general | solution.py:17
  891.5 19.1 %multiply_subtract_fusion.2 = (f32[4,128,32,128]{3,1,2,0:T(8,128)}, f32[4,128,32,128]{3,1,2,0:T(8,128)}) fusion(f32[32,128]{1,0:T(8,128)S(1)} %copy-done.8, f32[32,128]{1,0:T(8,128)S(1)} %copy-done.9, f32[4,128,32,256]{3,1,2,0:T(8,128)} %fusion.37, f32[4,128,32,256]{3,1,2,0:T(8,128)} %fusion.39), kind=kLoop, calls=%fused_computation.70 | loop fusion | flops 16777216 | bytes 50364416 | tf_op jit(solution)/shard_map/sub | solution.py:40
  910.6 11.9 pad_maximum_fusion.3
  922.5 33.5 %fusion.14 = f32[4,128,64,128]{3,2,1,0:T(8,128)} fusion(f32[4,128,64,128]{3,1,2,0:T(8,128)} %pad_maximum_fusion.3, f32[32,32]{0,1:T(8,128)S(1)} %copy-done.6, f32[32,32]{0,1:T(8,128)S(1)} %copy-done.14, f32[32,32]{0,1:T(8,128)S(1)} %copy-done.4), kind=kOutput, calls=%fused_computation.38 | convolution fusion | flops 3221237760 | bytes 33566720 | tf_op jit(solution)/shard_map/...pk,pj->...jk/dot_general | solution.py:21
  956.0 11.1 fusion.111
  967.1 7.9 copy.253
  980.0 7.9 copy.254
  987.9 175.7 %all-to-all-done.5 = f32[4,128,4096]{1,0,2:T(4,128)} async-done(((f32[4,128,4096]{1,0,2:T(4,128)}), f32[4,128,4096]{1,0,2:T(4,128)}, u32[]{:S(2)}, u32[]{:S(2)}) %all-to-all-start.5) | async-done | bytes 8388640 | tf_op jit(solution)/shard_map/all_to_all | solution.py:117
  1170.8 8.7 copy.220
  1179.5 10.4 copy.221
  1189.9 18.5 %all_to_all.167 = f32[4,1024,512]{1,0,2:T(4,128)} all-to-all(f32[4,1024,512]{1,0,2:T(4,128)} %copy.221), channel_id=1, replica_groups=mesh['tiles'=2,'row'=8,'col'=2] {'col'}, dimensions={2} | all-to-all | bytes 16777216 | tf_op jit(solution)/shard_map/all_to_all | solution.py:116
  1213.5 11.5 copy.222
  1225.1 8.7 copy.223
  1233.8 7.6 copy.224
  1241.4 155.6 %all-to-all-done.7 = f32[4,128,4096]{1,0,2:T(4,128)} async-done(((f32[4,128,4096]{1,0,2:T(4,128)}), f32[4,128,4096]{1,0,2:T(4,128)}, u32[]{:S(2)}, u32[]{:S(2)}) %all-to-all-start.7) | async-done | bytes 8388640 | tf_op jit(solution)/shard_map/all_to_all | solution.py:124
  1397.0 7.3 copy.227
  1404.3 8.7 copy.228
  1413.1 10.4 copy.229
  1423.4 12.2 all_to_all.168
  1435.7 8.3 copy.230
  1443.9 8.7 copy.231
  1456.7 31.3 %fusion.33 = f32[4,256,32,256]{3,1,2,0:T(8,128)} fusion(f32[4,256,64,32]{1,3,2,0:T(8,128)S(1)} %bitcast.141, f32[64,128]{1,0:T(8,128)S(1)} %get-tuple-element.49, f32[64,128]{1,0:T(8,128)S(1)} %get-tuple-element.50), kind=kOutput, calls=%fused_computation.57 | convolution fusion | flops 6442467328 | bytes 42008576 | tf_op jit(solution)/shard_map/...qp,qk->...pk/dot_general | solution.py:17
  1488.1 31.5 %fusion.35 = f32[4,256,32,256]{3,1,2,0:T(8,128)} fusion(f32[4,256,64,32]{1,3,2,0:T(8,128)S(1)} %bitcast.140, f32[64,128]{1,0:T(8,128)S(1)} %get-tuple-element.49, f32[64,128]{1,0:T(8,128)S(1)} %get-tuple-element.50), kind=kOutput, calls=%fused_computation.59 | convolution fusion | flops 6442467328 | bytes 42008576 | tf_op jit(solution)/shard_map/...qp,qk->...pk/dot_general | solution.py:17
  1519.6 34.7 %multiply_subtract_fusion = (f32[4,256,32,128]{3,1,2,0:T(8,128)}, f32[4,256,32,128]{3,1,2,0:T(8,128)}) fusion(f32[32,128]{1,0:T(8,128)S(1)} %copy-done.8, f32[32,128]{1,0:T(8,128)S(1)} %copy-done.9, f32[4,256,32,256]{3,1,2,0:T(8,128)} %fusion.33, f32[4,256,32,256]{3,1,2,0:T(8,128)} %fusion.35), kind=kLoop, calls=%fused_computation.16 | loop fusion | flops 33554432 | bytes 100696064 | tf_op jit(solution)/shard_map/sub | solution.py:40
  1554.3 23.3 %pad_maximum_fusion.1 = f32[4,256,64,128]{3,1,2,0:T(8,128)} fusion(f32[4,256,32,128]{3,1,2,0:T(8,128)} %get-tuple-element.6, f32[4,256,32,128]{3,1,2,0:T(8,128)} %get-tuple-element.5), kind=kLoop, calls=%fused_computation.1 | loop fusion | flops 8388608 | bytes 67108864 | tf_op jit(solution)/shard_map/concatenate | solution.py:42
  1577.6 47.1 %multiply_bitcast_fusion = f32[4,256,32,128]{3,2,1,0:T(8,128)} fusion(f32[4,256,64,128]{3,1,2,0:T(8,128)} %pad_maximum_fusion.1, f32[32,32]{0,1:T(8,128)S(1)} %copy-done.5, f32[32,32]{0,1:T(8,128)S(1)} %copy-done.7), kind=kOutput, calls=%fused_computation.14 | convolution fusion | flops 3225421824 | bytes 50339840 | tf_op jit(solution)/shard_map/...pk,pj->...jk/dot_general | solution.py:21
  1624.7 15.5 copy.255
  1640.2 31.6 %all_to_all.169 = f32[4,256,4096]{1,0,2:T(4,128)} all-to-all(f32[4,256,4096]{1,0,2:T(4,128)} %bitcast.136), channel_id=1, replica_groups=mesh['tiles'=2,'row'=8,'col'=2] {'col'}, dimensions={2} | all-to-all | bytes 33554432 | tf_op jit(solution)/shard_map/all_to_all | solution.py:135
  1671.8 19.2 %copy.236 = f32[4,2,256,2048]{3,2,1,0:T(8,128)} copy(f32[4,2,256,2048]{2,0,3,1:T(4,128)} %bitcast.137) | data formatting | bytes 33554432 | tf_op jit(solution)/shard_map/all_to_all | solution.py:135
  (71 shorter events, 125.5 us)
Async XLA Ops:
  20.9 23.2 %all-to-all-start = ((f32[4,512,2048]{2,0,1:T(4,128)}), f32[4,512,2048]{2,0,1:T(4,128)}, u32[]{:S(2)}, u32[]{:S(2)}) async-start(f32[4,512,2048]{2,0,1:T(4,128)} %copy.174), calls=%async_computation | async-start | bytes 33554432 | tf_op jit(solution)/shard_map/all_to_all | solution.py:71
  30.9 91.5 %copy-start.10 = (f32[32,128]{1,0:T(8,128)}, f32[32,128]{1,0:T(8,128)S(1)}, u32[]{:S(2)}) copy-start(f32[32,128]{1,0:T(8,128)S(1)} %get-tuple-element.37) | copy-start | bytes 49156
  30.9 91.5 %copy-start.12 = (f32[32,128]{1,0:T(8,128)}, f32[32,128]{1,0:T(8,128)S(1)}, u32[]{:S(2)}) copy-start(f32[32,128]{1,0:T(8,128)S(1)} %get-tuple-element.38) | copy-start | bytes 49156
  31.2 47.1 %copy-start = (f32[128,128]{0,1:T(8,128)}, f32[128,128]{0,1:T(8,128)S(1)}, u32[]{:S(2)}) copy-start(f32[128,128]{0,1:T(8,128)S(1)} %get-tuple-element.35) | copy-start | bytes 196612
  31.2 47.1 %copy-start.2 = (f32[128,128]{0,1:T(8,128)}, f32[128,128]{0,1:T(8,128)S(1)}, u32[]{:S(2)}) copy-start(f32[128,128]{0,1:T(8,128)S(1)} %get-tuple-element.36) | copy-start | bytes 196612
  229.5 190.7 %all-to-all-start.1 = ((f32[4,256,2048]{1,0,2:T(4,128)}), f32[4,256,2048]{1,0,2:T(4,128)}, u32[]{:S(2)}, u32[]{:S(2)}) async-start(f32[4,256,2048]{1,0,2:T(4,128)} %bitcast.144), calls=%async_computation.1 | async-start | bytes 16777216 | tf_op jit(solution)/shard_map/all_to_all | solution.py:81
  466.1 188.8 %all-to-all-start.3 = ((f32[4,256,2048]{1,0,2:T(4,128)}), f32[4,256,2048]{1,0,2:T(4,128)}, u32[]{:S(2)}, u32[]{:S(2)}) async-start(f32[4,256,2048]{1,0,2:T(4,128)} %bitcast.142), calls=%async_computation.3 | async-start | bytes 16777216 | tf_op jit(solution)/shard_map/all_to_all | solution.py:88
  567.8 4.0 copy-start.1
  567.8 4.0 copy-start.3
  715.7 19.6 %copy-start.11 = (f32[32,128]{1,0:T(8,128)S(1)}, f32[32,128]{1,0:T(8,128)}, u32[]{:S(2)}) copy-start(f32[32,128]{1,0:T(8,128)} %copy-done.10) | copy-start | bytes 49156
  715.7 19.6 %copy-start.13 = (f32[32,128]{1,0:T(8,128)S(1)}, f32[32,128]{1,0:T(8,128)}, u32[]{:S(2)}) copy-start(f32[32,128]{1,0:T(8,128)} %copy-done.12) | copy-start | bytes 49156
  871.9 19.5 %copy-start.8 = (f32[32,128]{1,0:T(8,128)S(1)}, f32[32,128]{1,0:T(8,128)}, u32[]{:S(2)}) copy-start(f32[32,128]{1,0:T(8,128)} %get-tuple-element.45) | copy-start | bytes 49156
  872.0 19.5 %copy-start.9 = (f32[32,128]{1,0:T(8,128)S(1)}, f32[32,128]{1,0:T(8,128)}, u32[]{:S(2)}) copy-start(f32[32,128]{1,0:T(8,128)} %get-tuple-element.46) | copy-start | bytes 49156
  910.6 11.9 copy-start.4
  910.6 11.9 copy-start.6
  910.6 11.9 copy-start.14
  975.0 188.6 %all-to-all-start.5 = ((f32[4,128,4096]{1,0,2:T(4,128)}), f32[4,128,4096]{1,0,2:T(4,128)}, u32[]{:S(2)}, u32[]{:S(2)}) async-start(f32[4,128,4096]{1,0,2:T(4,128)} %bitcast.145), calls=%async_computation.5 | async-start | bytes 16777216 | tf_op jit(solution)/shard_map/all_to_all | solution.py:117
  1208.4 188.6 %all-to-all-start.7 = ((f32[4,128,4096]{1,0,2:T(4,128)}), f32[4,128,4096]{1,0,2:T(4,128)}, u32[]{:S(2)}, u32[]{:S(2)}) async-start(f32[4,128,4096]{1,0,2:T(4,128)} %bitcast.143), calls=%async_computation.7 | async-start | bytes 16777216 | tf_op jit(solution)/shard_map/all_to_all | solution.py:124
  1452.6 35.5 %slice-start = ((s8[8388608]{0:T(1024)(128)(4,1)}), s8[4194304]{0:T(1024)(128)(4,1)S(1)}, s32[]{:S(2)}) async-start(s8[8388608]{0:T(1024)(128)(4,1)} %bitcast.138), calls=%async_computation.10 | async-start | bytes 8388608
  1456.7 31.3 %slice-start.1 = ((s8[8388608]{0:T(1024)(128)(4,1)}), s8[4194304]{0:T(1024)(128)(4,1)S(1)}, s32[]{:S(2)}) async-start(s8[8388608]{0:T(1024)(128)(4,1)} %bitcast.138), calls=%async_computation.11 | async-start | bytes 8388608
  1554.3 23.3 %copy-start.5 = (f32[32,32]{0,1:T(8,128)S(1)}, f32[32,32]{0,1:T(8,128)}, u32[]{:S(2)}) copy-start(f32[32,32]{0,1:T(8,128)} %fusion.94) | copy-start | bytes 12292
  1554.3 23.3 %copy-start.7 = (f32[32,32]{0,1:T(8,128)S(1)}, f32[32,32]{0,1:T(8,128)}, u32[]{:S(2)}) copy-start(f32[32,32]{0,1:T(8,128)} %get-tuple-element.48) | copy-start | bytes 12292
where the time goes:
time: 1700 us; the launch traced here: 1690 us
  waiting for transfers between devices  583 us (34%)
  local copies, waits for them, and re-layouts  482 us (28%)
  matrix products  323 us (19%)
  other arithmetic  177 us (10%)
  blocking collectives  93.3 us (5%)
  starting transfers between devices  32.1 us (2%)
    dot_general x7, matrix products, contract_first(): jnp.einsum('...qp,qk->...pk', values, table, precision=lax.Precision.HIGH...  185 us
    all_to_all x1, waiting for transfers between devices, shards(): lax.all_to_all(back_real, 'row', split_axis=2, concat_axis=1, tiled=True)  176 us
    all_to_all x1, waiting for transfers between devices, shards(): lax.all_to_all(spec_real, 'row', split_axis=2, concat_axis=1, tiled=True)  175 us
    all_to_all x1, waiting for transfers between devices, shards(): lax.all_to_all(back_imag, 'row', split_axis=2, concat_axis=1, tiled=True)  156 us
    dot_general x4, matrix products, contract_second(): jnp.einsum('...pk,pj->...jk', values, table, precision=lax.Precision.HIGH...  138 us
    sub x4, other arithmetic, fourier(): turned_real = part_real * twist_cos - part_imag * twist_sin  90.5 us
    unnamed x43, local copies, waits for them, and re-layouts  71.9 us
    concatenate x4, other arithmetic, fourier(): stacked = jnp.concatenate([turned_real, turned_imag], axis=-2)  65.5 us
  transfers between devices with their start and end apart: 5, of which 5 were waited for; matrix products, arithmetic and copies ran while one was open for 10% of the time, Pallas kernels for 0%

commit v1 on v0

--- a/solution.py
+++ b/solution.py
@@ -84,12 +84,20 @@
             concat_axis=1,
             tiled=True,
         ),
-        lax.all_to_all(
-            lax.all_to_all(spec_imag, "row", split_axis=2, concat_axis=1, tiled=True),
-            "col",
-            split_axis=2,
-            concat_axis=1,
-            tiled=True,
+        jnp.concatenate(
+            lax.all_to_all(
+                jnp.stack(
+                    jnp.split(
+                        lax.all_to_all(spec_imag, "row", split_axis=2, concat_axis=1, tiled=True),
+                        lax.axis_size("col"),
+                        axis=2,
+                    )
+                ),
+                "col",
+                0,
+                0,
+            ),
+            axis=1,
         ),
     )
     line_real = reorder_blocks(moved_real, row_count, col_count)

time: 1700 us -> 1680 us (0.988)
  local copies, waits for them, and re-layouts: 482 us -> 456 us
where the time goes in v1:
time: 1680 us; the launch traced here: 1660 us
  waiting for transfers between devices  583 us (35%)
  local copies, waits for them, and re-layouts  456 us (27%)
  matrix products  323 us (19%)
  other arithmetic  178 us (11%)
  blocking collectives  91.7 us (5%)
  starting transfers between devices  32.1 us (2%)
    dot_general x7, matrix products, contract_first(): jnp.einsum('...qp,qk->...pk', values, table, precision=lax.Precision.HIGH...  185 us
    all_to_all x1, waiting for transfers between devices, shards(): lax.all_to_all(back_real, 'row', split_axis=2, concat_axis=1, tiled=True)  176 us
    all_to_all x1, waiting for transfers between devices, shards(): lax.all_to_all(spec_real, 'row', split_axis=2, concat_axis=1, tiled=True)  175 us
    all_to_all x1, waiting for transfers between devices, shards(): lax.all_to_all(back_imag, 'row', split_axis=2, concat_axis=1, tiled=True)  156 us
    dot_general x4, matrix products, contract_second(): jnp.einsum('...pk,pj->...jk', values, table, precision=lax.Precision.HIGH...  138 us
    sub x4, other arithmetic, fourier(): turned_real = part_real * twist_cos - part_imag * twist_sin  90.6 us
    unnamed x43, local copies, waits for them, and re-layouts  71.9 us
    concatenate x4, other arithmetic, fourier(): stacked = jnp.concatenate([turned_real, turned_imag], axis=-2)  65.7 us
  transfers between devices with their start and end apart: 5, of which 5 were waited for; matrix products, arithmetic and copies ran while one was open for 10% of the time, Pallas kernels for 0%

profile of v1, /device:TPU:0, one launch (start us, length us, event | category | flops | bytes accessed | tf_op | source)
XLA Modules:
  0.0 1664.7 jit_solution(13805459004806867108)
XLA Ops:
  0.0 20.9 %copy.173 = f32[4,512,2048]{2,0,1:T(4,128)} copy(f32[4,512,2048]{2,1,0:T(8,128)} %param.2) | data formatting | bytes 33554432 | tf_op args[0]
  20.9 9.7 all-to-all-start
  31.2 12.9 all-to-all-done
  44.1 17.8 %copy.174 = f32[4,512,2048]{2,1,0:T(8,128)} copy(f32[4,512,2048]{2,0,1:T(4,128)} %all-to-all-done) | data formatting | bytes 33554432 | tf_op jit(solution)/shard_map/all_to_all | solution.py:71
  61.9 16.4 copy.175
  78.3 44.1 %fusion.8 = f32[4,256,32,256]{1,3,2,0:T(8,128)} fusion(f32[4,256,128,32]{1,3,2,0:T(8,128)} %bitcast.137, f32[128,128]{0,1:T(8,128)S(1)} %get-tuple-element.37, f32[128,128]{0,1:T(8,128)S(1)} %get-tuple-element.38), kind=kOutput, calls=%fused_computation.19 | convolution fusion | flops 12884934656 | bytes 50462720 | tf_op jit(solution)/shard_map/...qp,qk->...pk/dot_general | solution.py:17
  122.4 17.6 %multiply_subtract_fusion.1 = (f32[4,256,32,128]{1,3,2,0:T(8,128)S(1)}, f32[4,256,32,128]{1,3,2,0:T(8,128)}) fusion(f32[4,256,32,256]{1,3,2,0:T(8,128)} %fusion.8, f32[32,128]{1,0:T(8,128)S(1)} %get-tuple-element.39, f32[32,128]{1,0:T(8,128)S(1)} %get-tuple-element.40), kind=kLoop, calls=%fused_computation.18 | loop fusion | flops 25165824 | bytes 67141632 | tf_op jit(solution)/shard_map/sub | solution.py:40
  140.0 18.6 %pad_maximum_fusion = f32[4,256,64,128]{1,3,2,0:T(8,128)} fusion(f32[4,256,32,128]{1,3,2,0:T(8,128)} %get-tuple-element.14, f32[4,256,32,128]{1,3,2,0:T(8,128)S(1)} %get-tuple-element.13), kind=kLoop, calls=%fused_computation | loop fusion | flops 8388608 | bytes 67108864 | tf_op jit(solution)/shard_map/concatenate | solution.py:42
  158.6 31.9 %copy.177 = f32[4,256,64,128]{3,2,1,0:T(8,128)} copy(f32[4,256,64,128]{1,3,2,0:T(8,128)} %pad_maximum_fusion) | data formatting | bytes 67108864 | tf_op jit(solution)/shard_map/concatenate | solution.py:42
  190.5 24.1 %convolution_bitcast_fusion = f32[4,256,32,128]{3,2,1,0:T(8,128)S(1)} fusion(f32[4,256,64,128]{3,2,1,0:T(8,128)} %copy.177, f32[32,16]{0,1:T(8,128)S(1)} %get-tuple-element.42, f32[32,16]{0,1:T(8,128)S(1)} %get-tuple-element.41, f32[32,16]{0,1:T(8,128)S(1)} %fusion.98), kind=kOutput, calls=%fused_computation.36 | convolution fusion | flops 3221231616 | bytes 50337792 | tf_op jit(solution)/shard_map/...pk,pj->...jk/dot_general | solution.py:21
  214.6 6.9 fusion.113
  221.5 8.1 copy.243
  229.6 7.3 all-to-all-start.1
  236.9 8.0 copy.245
  244.9 175.5 %all-to-all-done.1 = f32[4,256,2048]{1,0,2:T(4,128)} async-done(((f32[4,256,2048]{1,0,2:T(4,128)}), f32[4,256,2048]{1,0,2:T(4,128)}, u32[]{:S(2)}, u32[]{:S(2)}) %all-to-all-start.1) | async-done | bytes 8388640 | tf_op jit(solution)/shard_map/all_to_all | solution.py:81
  420.4 8.2 copy.179
  428.6 8.7 copy.180
  437.3 10.4 copy.181
  447.7 18.5 %all_to_all.155 = f32[4,2048,256]{1,0,2:T(4,128)} all-to-all(f32[4,2048,256]{1,0,2:T(4,128)} %copy.181), channel_id=1, replica_groups=mesh['tiles'=2,'row'=8,'col'=2] {'col'}, dimensions={2} | all-to-all | bytes 16777216 | tf_op jit(solution)/shard_map/all_to_all | solution.py:80
  471.4 23.0 %fusion.110 = (bf16[1,4,1,128,4096]{4,3,2,1,0:T(8,128)(2,1)}, bf16[1,4,1,128,4096]{4,3,2,1,0:T(8,128)(2,1)}, bf16[1,4,1,128,4096]{4,3,2,1,0:T(8,128)(2,1)}, bf16...) fusion(bf16[2,4,4,128,4096]{4,3,2,1,0:T(8,128)(2,1)} %param.3), kind=kLoop, calls=%fused_computation.175 | loop fusion | bytes 67108864 | tf_op jit(solution)/shard_map/slice | solution.py:110
  547.8 11.5 copy.182
  559.3 8.7 copy.183
  572.0 19.7 %fusion.43 = f32[4,128,32,256]{3,1,2,0:T(8,128)} fusion(f32[4,128,128,32]{1,3,2,0:T(8,128)S(1)} %bitcast.136, f32[128,128]{0,1:T(8,128)S(1)} %copy-done.1, f32[128,128]{0,1:T(8,128)S(1)} %copy-done.3), kind=kOutput, calls=%fused_computation.68 | convolution fusion | flops 6442483712 | bytes 25296896 | tf_op jit(solution)/shard_map/...qp,qk->...pk/dot_general | solution.py:17
  591.6 63.4 %all-to-all-done.3 = f32[4,256,2048]{1,0,2:T(4,128)} async-done(((f32[4,256,2048]{1,0,2:T(4,128)}), f32[4,256,2048]{1,0,2:T(4,128)}, u32[]{:S(2)}, u32[]{:S(2)}) %all-to-all-start.3) | async-done | bytes 8388640 | tf_op jit(solution)/shard_map/all_to_all | solution.py:91
  655.0 8.4 copy.188
  663.4 8.7 copy.189
  676.7 10.9 all_to_all.156
  688.6 19.5 %fusion.41 = f32[4,128,32,256]{3,1,2,0:T(8,128)} fusion(f32[4,128,128,32]{1,3,2,0:T(8,128)S(1)} %bitcast.135, f32[128,128]{0,1:T(8,128)S(1)} %copy-done.1, f32[128,128]{0,1:T(8,128)S(1)} %copy-done.3), kind=kOutput, calls=%fused_computation.66 | convolution fusion | flops 6442483712 | bytes 25296896 | tf_op jit(solution)/shard_map/...qp,qk->...pk/dot_general | solution.py:17
  708.2 19.1 %multiply_subtract_fusion.3 = (f32[4,128,32,128]{3,1,2,0:T(8,128)}, f32[4,128,32,128]{3,1,2,0:T(8,128)}) fusion(f32[32,128]{1,0:T(8,128)S(1)} %copy-done.11, f32[32,128]{1,0:T(8,128)S(1)} %copy-done.13, f32[4,128,32,256]{3,1,2,0:T(8,128)} %fusion.41, f32[4,128,32,256]{3,1,2,0:T(8,128)} %fusion.43), kind=kLoop, calls=%fused_computation.73 | loop fusion | flops 16777216 | bytes 50364416 | tf_op jit(solution)/shard_map/sub | solution.py:40
  727.3 11.9 pad_maximum_fusion.2
  739.1 33.5 %fusion.11 = f32[4,128,64,128]{3,2,1,0:T(8,128)} fusion(f32[4,128,64,128]{3,1,2,0:T(8,128)} %pad_maximum_fusion.2, f32[32,32]{0,1:T(8,128)S(1)} %get-tuple-element.44, f32[32,32]{0,1:T(8,128)S(1)} %get-tuple-element.43, f32[32,32]{0,1:T(8,128)S(1)} %fusion.95), kind=kOutput, calls=%fused_computation.37 | convolution fusion | flops 3221237760 | bytes 33566720 | tf_op jit(solution)/shard_map/...pk,pj->...jk/dot_general | solution.py:21
  772.6 12.2 fusion.112
  807.8 17.6 %fusion.22 = (f32[4,128,128,32]{1,3,2,0:T(8,128)S(1)}, f32[4,128,128,32]{1,3,2,0:T(8,128)S(1)}) fusion(bf16[4,128,128,32]{1,3,2,0:T(8,128)(2,1)} %bitcast.171, bf16[4,128,128,32]{1,3,2,0:T(8,128)(2,1)} %bitcast.170, bf16[4,128,128,32]{1,3,2,0:T(8,128)(2,1)} %bitcast.169, bf16[4,128,128,32]{1,3,2,0:T(8,128)(2,1)} %bitcast.168, ...), kind=kLoop, calls=%fused_computation.42 | loop fusion | flops 79691776 | bytes 67108864 | tf_op jit(solution)/shard_map/add | solution.py:119
  825.4 19.4 %fusion.39 = f32[4,128,32,256]{3,1,2,0:T(8,128)} fusion(f32[4,128,128,32]{1,3,2,0:T(8,128)S(1)} %get-tuple-element.7, f32[128,128]{0,1:T(8,128)S(1)} %get-tuple-element.45, f32[128,128]{0,1:T(8,128)S(1)} %get-tuple-element.46), kind=kOutput, calls=%fused_computation.64 | convolution fusion | flops 6442483712 | bytes 25296896 | tf_op jit(solution)/shard_map/...qp,qk->...pk/dot_general | solution.py:17
  844.9 19.5 %fusion.37 = f32[4,128,32,256]{3,1,2,0:T(8,128)} fusion(f32[4,128,128,32]{1,3,2,0:T(8,128)S(1)} %get-tuple-element.8, f32[128,128]{0,1:T(8,128)S(1)} %get-tuple-element.45, f32[128,128]{0,1:T(8,128)S(1)} %get-tuple-element.46), kind=kOutput, calls=%fused_computation.62 | convolution fusion | flops 6442483712 | bytes 25296896 | tf_op jit(solution)/shard_map/...qp,qk->...pk/dot_general | solution.py:17
  864.4 19.1 %multiply_subtract_fusion.2 = (f32[4,128,32,128]{3,1,2,0:T(8,128)}, f32[4,128,32,128]{3,1,2,0:T(8,128)}) fusion(f32[32,128]{1,0:T(8,128)S(1)} %copy-done.8, f32[32,128]{1,0:T(8,128)S(1)} %copy-done.9, f32[4,128,32,256]{3,1,2,0:T(8,128)} %fusion.37, f32[4,128,32,256]{3,1,2,0:T(8,128)} %fusion.39), kind=kLoop, calls=%fused_computation.71 | loop fusion | flops 16777216 | bytes 50364416 | tf_op jit(solution)/shard_map/sub | solution.py:40
  883.6 11.9 pad_maximum_fusion.3
  895.4 33.5 %fusion.14 = f32[4,128,64,128]{3,2,1,0:T(8,128)} fusion(f32[4,128,64,128]{3,1,2,0:T(8,128)} %pad_maximum_fusion.3, f32[32,32]{0,1:T(8,128)S(1)} %copy-done.6, f32[32,32]{0,1:T(8,128)S(1)} %copy-done.14, f32[32,32]{0,1:T(8,128)S(1)} %copy-done.4), kind=kOutput, calls=%fused_computation.38 | convolution fusion | flops 3221237760 | bytes 33566720 | tf_op jit(solution)/shard_map/...pk,pj->...jk/dot_general | solution.py:21
  929.0 11.1 fusion.111
  940.1 7.9 copy.249
  952.9 7.9 copy.250
  960.9 175.7 %all-to-all-done.5 = f32[4,128,4096]{1,0,2:T(4,128)} async-done(((f32[4,128,4096]{1,0,2:T(4,128)}), f32[4,128,4096]{1,0,2:T(4,128)}, u32[]{:S(2)}, u32[]{:S(2)}) %all-to-all-start.5) | async-done | bytes 8388640 | tf_op jit(solution)/shard_map/all_to_all | solution.py:125
  1136.6 7.2 copy.215
  1143.7 8.7 copy.216
  1152.4 10.4 copy.217
  1162.9 18.5 %all_to_all.157 = f32[4,1024,512]{1,0,2:T(4,128)} all-to-all(f32[4,1024,512]{1,0,2:T(4,128)} %copy.217), channel_id=1, replica_groups=mesh['tiles'=2,'row'=8,'col'=2] {'col'}, dimensions={2} | all-to-all | bytes 16777216 | tf_op jit(solution)/shard_map/all_to_all | solution.py:124
  1186.5 11.5 copy.218
  1198.0 8.7 copy.219
  1206.7 7.6 copy.220
  1214.3 155.6 %all-to-all-done.7 = f32[4,128,4096]{1,0,2:T(4,128)} async-done(((f32[4,128,4096]{1,0,2:T(4,128)}), f32[4,128,4096]{1,0,2:T(4,128)}, u32[]{:S(2)}, u32[]{:S(2)}) %all-to-all-start.7) | async-done | bytes 8388640 | tf_op jit(solution)/shard_map/all_to_all | solution.py:132
  1370.0 7.3 copy.223
  1377.3 8.7 copy.224
  1386.0 10.4 copy.225
  1396.4 12.2 all_to_all.158
  1408.6 8.3 copy.226
  1416.9 8.7 copy.227
  1429.7 31.4 %fusion.33 = f32[4,256,32,256]{3,1,2,0:T(8,128)} fusion(f32[4,256,64,32]{1,3,2,0:T(8,128)S(1)} %bitcast.144, f32[64,128]{1,0:T(8,128)S(1)} %get-tuple-element.51, f32[64,128]{1,0:T(8,128)S(1)} %get-tuple-element.52), kind=kOutput, calls=%fused_computation.58 | convolution fusion | flops 6442467328 | bytes 42008576 | tf_op jit(solution)/shard_map/...qp,qk->...pk/dot_general | solution.py:17
  1461.1 31.6 %fusion.35 = f32[4,256,32,256]{3,1,2,0:T(8,128)} fusion(f32[4,256,64,32]{1,3,2,0:T(8,128)S(1)} %bitcast.143, f32[64,128]{1,0:T(8,128)S(1)} %get-tuple-element.51, f32[64,128]{1,0:T(8,128)S(1)} %get-tuple-element.52), kind=kOutput, calls=%fused_computation.60 | convolution fusion | flops 6442467328 | bytes 42008576 | tf_op jit(solution)/shard_map/...qp,qk->...pk/dot_general | solution.py:17
  1492.7 34.7 %multiply_subtract_fusion = (f32[4,256,32,128]{3,1,2,0:T(8,128)}, f32[4,256,32,128]{3,1,2,0:T(8,128)}) fusion(f32[32,128]{1,0:T(8,128)S(1)} %copy-done.8, f32[32,128]{1,0:T(8,128)S(1)} %copy-done.9, f32[4,256,32,256]{3,1,2,0:T(8,128)} %fusion.33, f32[4,256,32,256]{3,1,2,0:T(8,128)} %fusion.35), kind=kLoop, calls=%fused_computation.16 | loop fusion | flops 33554432 | bytes 100696064 | tf_op jit(solution)/shard_map/sub | solution.py:40
  1527.5 23.3 %pad_maximum_fusion.1 = f32[4,256,64,128]{3,1,2,0:T(8,128)} fusion(f32[4,256,32,128]{3,1,2,0:T(8,128)} %get-tuple-element.6, f32[4,256,32,128]{3,1,2,0:T(8,128)} %get-tuple-element.5), kind=kLoop, calls=%fused_computation.1 | loop fusion | flops 8388608 | bytes 67108864 | tf_op jit(solution)/shard_map/concatenate | solution.py:42
  1550.8 47.1 %multiply_bitcast_fusion = f32[4,256,32,128]{3,2,1,0:T(8,128)} fusion(f32[4,256,64,128]{3,1,2,0:T(8,128)} %pad_maximum_fusion.1, f32[32,32]{0,1:T(8,128)S(1)} %copy-done.5, f32[32,32]{0,1:T(8,128)S(1)} %copy-done.7), kind=kOutput, calls=%fused_computation.14 | convolution fusion | flops 3225421824 | bytes 50339840 | tf_op jit(solution)/shard_map/...pk,pj->...jk/dot_general | solution.py:21
  1597.9 15.5 copy.251
  1613.4 31.6 %all_to_all.159 = f32[4,256,4096]{1,0,2:T(4,128)} all-to-all(f32[4,256,4096]{1,0,2:T(4,128)} %bitcast.139), channel_id=1, replica_groups=mesh['tiles'=2,'row'=8,'col'=2] {'col'}, dimensions={2} | all-to-all | bytes 33554432 | tf_op jit(solution)/shard_map/all_to_all | solution.py:143
  1645.1 19.2 %copy.232 = f32[4,2,256,2048]{3,2,1,0:T(8,128)} copy(f32[4,2,256,2048]{2,0,3,1:T(4,128)} %bitcast.140) | data formatting | bytes 33554432 | tf_op jit(solution)/shard_map/all_to_all | solution.py:143
  (70 shorter events, 105.8 us)
Async XLA Ops:
  20.9 23.2 %all-to-all-start = ((f32[4,512,2048]{2,0,1:T(4,128)}), f32[4,512,2048]{2,0,1:T(4,128)}, u32[]{:S(2)}, u32[]{:S(2)}) async-start(f32[4,512,2048]{2,0,1:T(4,128)} %copy.173), calls=%async_computation | async-start | bytes 33554432 | tf_op jit(solution)/shard_map/all_to_all | solution.py:71
  30.9 91.5 %copy-start.10 = (f32[32,128]{1,0:T(8,128)}, f32[32,128]{1,0:T(8,128)S(1)}, u32[]{:S(2)}) copy-start(f32[32,128]{1,0:T(8,128)S(1)} %get-tuple-element.39) | copy-start | bytes 49156
  30.9 91.5 %copy-start.12 = (f32[32,128]{1,0:T(8,128)}, f32[32,128]{1,0:T(8,128)S(1)}, u32[]{:S(2)}) copy-start(f32[32,128]{1,0:T(8,128)S(1)} %get-tuple-element.40) | copy-start | bytes 49156
  31.2 47.1 %copy-start = (f32[128,128]{0,1:T(8,128)}, f32[128,128]{0,1:T(8,128)S(1)}, u32[]{:S(2)}) copy-start(f32[128,128]{0,1:T(8,128)S(1)} %get-tuple-element.37) | copy-start | bytes 196612
  31.2 47.1 %copy-start.2 = (f32[128,128]{0,1:T(8,128)}, f32[128,128]{0,1:T(8,128)S(1)}, u32[]{:S(2)}) copy-start(f32[128,128]{0,1:T(8,128)S(1)} %get-tuple-element.38) | copy-start | bytes 196612
  229.6 190.7 %all-to-all-start.1 = ((f32[4,256,2048]{1,0,2:T(4,128)}), f32[4,256,2048]{1,0,2:T(4,128)}, u32[]{:S(2)}, u32[]{:S(2)}) async-start(f32[4,256,2048]{1,0,2:T(4,128)} %bitcast.147), calls=%async_computation.1 | async-start | bytes 16777216 | tf_op jit(solution)/shard_map/all_to_all | solution.py:81
  466.2 188.8 %all-to-all-start.3 = ((f32[4,256,2048]{1,0,2:T(4,128)}), f32[4,256,2048]{1,0,2:T(4,128)}, u32[]{:S(2)}, u32[]{:S(2)}) async-start(f32[4,256,2048]{1,0,2:T(4,128)} %bitcast.145), calls=%async_computation.3 | async-start | bytes 16777216 | tf_op jit(solution)/shard_map/all_to_all | solution.py:91
  568.0 4.0 copy-start.1
  568.0 4.0 copy-start.3
  688.6 19.6 %copy-start.11 = (f32[32,128]{1,0:T(8,128)S(1)}, f32[32,128]{1,0:T(8,128)}, u32[]{:S(2)}) copy-start(f32[32,128]{1,0:T(8,128)} %copy-done.10) | copy-start | bytes 49156
  688.6 19.6 %copy-start.13 = (f32[32,128]{1,0:T(8,128)S(1)}, f32[32,128]{1,0:T(8,128)}, u32[]{:S(2)}) copy-start(f32[32,128]{1,0:T(8,128)} %copy-done.12) | copy-start | bytes 49156
  844.9 19.5 %copy-start.8 = (f32[32,128]{1,0:T(8,128)S(1)}, f32[32,128]{1,0:T(8,128)}, u32[]{:S(2)}) copy-start(f32[32,128]{1,0:T(8,128)} %get-tuple-element.47) | copy-start | bytes 49156
  844.9 19.5 %copy-start.9 = (f32[32,128]{1,0:T(8,128)S(1)}, f32[32,128]{1,0:T(8,128)}, u32[]{:S(2)}) copy-start(f32[32,128]{1,0:T(8,128)} %get-tuple-element.48) | copy-start | bytes 49156
  883.5 11.9 copy-start.4
  883.5 11.9 copy-start.6
  883.5 11.9 copy-start.14
  947.9 188.6 %all-to-all-start.5 = ((f32[4,128,4096]{1,0,2:T(4,128)}), f32[4,128,4096]{1,0,2:T(4,128)}, u32[]{:S(2)}, u32[]{:S(2)}) async-start(f32[4,128,4096]{1,0,2:T(4,128)} %bitcast.148), calls=%async_computation.5 | async-start | bytes 16777216 | tf_op jit(solution)/shard_map/all_to_all | solution.py:125
  1181.3 188.6 %all-to-all-start.7 = ((f32[4,128,4096]{1,0,2:T(4,128)}), f32[4,128,4096]{1,0,2:T(4,128)}, u32[]{:S(2)}, u32[]{:S(2)}) async-start(f32[4,128,4096]{1,0,2:T(4,128)} %bitcast.146), calls=%async_computation.7 | async-start | bytes 16777216 | tf_op jit(solution)/shard_map/all_to_all | solution.py:132
  1425.6 35.6 %slice-start = ((s8[8388608]{0:T(1024)(128)(4,1)}), s8[4194304]{0:T(1024)(128)(4,1)S(1)}, s32[]{:S(2)}) async-start(s8[8388608]{0:T(1024)(128)(4,1)} %bitcast.141), calls=%async_computation.10 | async-start | bytes 8388608
  1429.7 31.5 %slice-start.1 = ((s8[8388608]{0:T(1024)(128)(4,1)}), s8[4194304]{0:T(1024)(128)(4,1)S(1)}, s32[]{:S(2)}) async-start(s8[8388608]{0:T(1024)(128)(4,1)} %bitcast.141), calls=%async_computation.11 | async-start | bytes 8388608
  1527.5 23.3 %copy-start.5 = (f32[32,32]{0,1:T(8,128)S(1)}, f32[32,32]{0,1:T(8,128)}, u32[]{:S(2)}) copy-start(f32[32,32]{0,1:T(8,128)} %fusion.94) | copy-start | bytes 12292
  1527.5 23.3 %copy-start.7 = (f32[32,32]{0,1:T(8,128)S(1)}, f32[32,32]{0,1:T(8,128)}, u32[]{:S(2)}) copy-start(f32[32,32]{0,1:T(8,128)} %get-tuple-element.50) | copy-start | bytes 12292
